TPU v7x, 32 devices: a whole 2x2x4 slice. The times are simulated.
32 devices in a mesh: leaf: 8 (over z, y), rhs: 4 (over x, core).
Axes of the slice: x: 2, y: 2, z: 4, core: 2. Of those that a mesh axis runs over, the one named last changes fastest.
Arguments:
- leaf_parents: int32 [32], replicated, may hold values from 0 to 15, as said below
- mid_parents: int32 [16], replicated, may hold values from 0 to 7, as said below
- leaf_codes: int32 [32, 1], replicated, may hold values from 0 to 7, as said below
- mid_codes: int32 [16, 1], replicated, may hold values from 0 to 3, as said below
- leaf_valid: int32 [32], P('leaf'), may hold values from 1 to 128
- mid_valid: int32 [16], P('leaf'), may hold values from 1 to 128
- leaf_inverse: bfloat16 [32, 512, 512], P('leaf')
- mid_inverse: bfloat16 [16, 512, 512], P('leaf')
- top_inverse: bfloat16 [8, 512, 512], P('leaf')
- leaf_panels: bfloat16 [32, 128, 512], P('leaf'), may hold values from -0.1875 to 0.1875
- mid_panels: bfloat16 [16, 128, 512], P('leaf'), may hold values from -0.1875 to 0.1875
- leaf_cotangent: bfloat16 [32, 128, 512], P('leaf', 'rhs'), may hold values from -6 to 6
- mid_cotangent: bfloat16 [16, 128, 512], P('leaf', 'rhs'), may hold values from -6 to 6
- top_cotangent: bfloat16 [8, 128, 512], P('leaf', 'rhs'), may hold values from -6 to 6
- mid_primal: bfloat16 [16, 128, 512], P('leaf', 'rhs'), may hold values from -0.59765625 to 0.59765625
- top_primal: bfloat16 [8, 128, 512], P('leaf', 'rhs'), may hold values from -0.59765625 to 0.59765625
Outputs:
- leaf_adjoint: bfloat16 [32, 128, 512], P('leaf', 'rhs')
- mid_adjoint: bfloat16 [16, 128, 512], P('leaf', 'rhs')
- top_adjoint: bfloat16 [8, 128, 512], P('leaf', 'rhs')
- leaf_grad: bfloat16 [32, 128, 512], P('leaf', 'rhs')
- mid_grad: bfloat16 [16, 128, 512], P('leaf', 'rhs')
Inputs may be any that keep to these rules, and one draw needn't show every extreme that they name: `leaf_parents`: the parent of level-0 supernode s is level-1 supernode s // 2 or one beside it. `mid_parents`: the parent of level-1 supernode p is level-2 supernode p // 2 or one beside it; it is p // 2 + 1 whenever p % 4 == 3 and p < 15. `leaf_codes`: the 1 codes of one panel are distinct. `mid_codes`: the 1 codes of one panel are distinct.
All inputs are finite; a program needn't handle non-finite values.
Results may differ from a plain program's by a relative error of at most 0.0053.
Values may be sent and summed in bfloat16 or wider, within the bound.
No kernel may reach another device: no remote copies, remote signals or barrier semaphores. Data moves between devices by JAX's collectives and lax.ppermute only.
A program may use at most 64 MiB of HBM per device.

v0:
```python
import jax
import jax.numpy as jnp
from jax import lax
from jax.sharding import PartitionSpec as P

BLK = 128
MR = 128
NB = 4


def padded(block, sides, width):
    for axis, dim in sides:
        count = lax.axis_size(axis)
        forward = [(i, i + 1) for i in range(count - 1)]
        backward = [(target, source) for source, target in forward]
        low = lax.ppermute(
            lax.slice_in_dim(block, block.shape[dim] - width, None, axis=dim), axis, forward
        )
        high = lax.ppermute(lax.slice_in_dim(block, 0, width, axis=dim), axis, backward)
        block = jnp.concatenate([low, block, high], axis=dim)
    return block


def from_behind(value, axis, by):
    peers = lax.axis_size(axis)
    pairs = [(i, i + by) for i in range(peers) if 0 <= i + by < peers]
    return lax.ppermute(value, axis, pairs)


def solve_level(block_rows, inverse):
    return lax.dot_general(
        block_rows, inverse, (((2,), (2,)), ((0,), (0,))), preferred_element_type=jnp.float32
    )


def mask_columns(block_rows, row_limit):
    columns = jnp.arange(block_rows.shape[2], dtype=jnp.int32)
    return jnp.where(
        columns[None, None, :] < row_limit[:, None, None], block_rows, jnp.zeros_like(block_rows)
    )


def panel_update(adjoint_rows, panel_block, row_limit):
    update = lax.dot_general(
        adjoint_rows, panel_block, (((2,), (2,)), ((0,), (0,))), preferred_element_type=jnp.float32
    )
    return mask_columns(update, row_limit)


def tile_grad(rows_block, adjoint_block):
    return -lax.dot_general(
        rows_block, adjoint_block, (((1,), (1,)), ((0,), (0,))), preferred_element_type=jnp.float32
    )


def table_pick(table, wanted):
    entries = table.shape[0]
    match = wanted[:, None] == jnp.arange(entries, dtype=jnp.int32)[None, :]
    extra = table.ndim - 1
    spread_match = match.reshape(match.shape + (1,) * extra)
    values = jnp.sum(jnp.where(spread_match, table[None], 0), axis=1)
    found = jnp.any(match, axis=1).reshape((wanted.shape[0],) + (1,) * extra)
    return jnp.where(found, values, -1)


def route_blocks(extended, targets, code_ids, own_nodes, offset):
    src_count = extended.shape[0]
    probe_count = extended.shape[1]
    code_count = code_ids.shape[1]
    block_width = extended.shape[2] // code_count
    blocks = jnp.arange(NB, dtype=jnp.int32)
    matched = (targets[None, :, None, None] == own_nodes[:, None, None, None]) & (
        code_ids[None, :, :, None] - offset == blocks[None, None, None, :]
    )
    weights = matched.astype(jnp.float32)
    pieces = extended.reshape(src_count, probe_count, code_count, block_width)
    placed = jnp.einsum("temb,enmc->tnbc", weights, pieces, precision=lax.Precision.HIGHEST)
    return placed.reshape(own_nodes.shape[0], probe_count, NB * block_width)


def pick_rows(extended, ext_ids, wanted, code_ids, offset):
    src_count = extended.shape[0]
    probe_count = extended.shape[1]
    blocks = jnp.arange(NB, dtype=jnp.int32)
    matched = (ext_ids[None, None, :, None] == wanted[:, None, None, None]) & (
        code_ids[:, :, None, None] - offset == blocks[None, None, None, :]
    )
    weights = matched.astype(jnp.bfloat16)
    pieces = extended.reshape(src_count, probe_count, NB, BLK)
    chosen = jnp.einsum("smeb,enbc->snmc", weights, pieces, preferred_element_type=jnp.float32)
    return chosen.reshape(wanted.shape[0], probe_count, MR)


def shards(
    leaf_parents,
    mid_parents,
    leaf_codes,
    mid_codes,
    leaf_valid,
    mid_valid,
    leaf_inverse,
    mid_inverse,
    top_inverse,
    leaf_panels,
    mid_panels,
    leaf_cotangent,
    mid_cotangent,
    top_cotangent,
    mid_primal,
    top_primal,
):
    leaf_count = leaf_inverse.shape[0]
    mid_count = mid_inverse.shape[0]
    top_count = top_inverse.shape[0]
    device = lax.axis_index("leaf")
    leaf_first = device * leaf_count
    mid_first = device * mid_count
    top_first = device * top_count
    own_mid_nodes = mid_first + jnp.arange(mid_count, dtype=jnp.int32)
    own_top_nodes = top_first + jnp.arange(top_count, dtype=jnp.int32)
    leaf_near_ids = leaf_first - leaf_count + jnp.arange(3 * leaf_count, dtype=jnp.int32)
    mid_near_ids = mid_first - mid_count + jnp.arange(3 * mid_count, dtype=jnp.int32)
    top_far_ids = top_first - 2 * top_count + jnp.arange(5 * top_count, dtype=jnp.int32)
    own_leaf_parents = lax.dynamic_slice_in_dim(leaf_parents, leaf_first, leaf_count, 0)
    own_leaf_codes = lax.dynamic_slice_in_dim(leaf_codes, leaf_first, leaf_count, 0)
    own_mid_parents = lax.dynamic_slice_in_dim(mid_parents, mid_first, mid_count, 0)
    own_mid_codes = lax.dynamic_slice_in_dim(mid_codes, mid_first, mid_count, 0)
    own_leaf_grand = table_pick(mid_parents, own_leaf_parents)
    near_mid_parents = table_pick(mid_parents, mid_near_ids)
    near_mid_codes = table_pick(mid_codes, mid_near_ids)
    parent_ext = padded(mid_primal, (("leaf", 0),), mid_count)
    grand_moved = [from_behind(top_primal, "leaf", step) for step in (2, 1, -1, -2)]
    grand_ext = jnp.concatenate(
        [grand_moved[0], grand_moved[1], top_primal, grand_moved[2], grand_moved[3]], axis=0
    )
    leaf_adjoint = solve_level(leaf_cotangent, leaf_inverse).astype(jnp.bfloat16)
    leaf_update = panel_update(leaf_adjoint, leaf_panels, leaf_valid)
    nearby = padded(leaf_update, (("leaf", 0),), leaf_count)
    near_parents = table_pick(leaf_parents, leaf_near_ids)
    near_codes = table_pick(leaf_codes, leaf_near_ids)
    to_middle = route_blocks(nearby, near_parents, near_codes, own_mid_nodes, 0)
    carried = route_blocks(nearby, near_parents, near_codes, own_mid_nodes, NB)
    middle_accum = mid_cotangent.astype(jnp.float32) - to_middle
    mid_adjoint = solve_level(middle_accum.astype(jnp.bfloat16), mid_inverse).astype(jnp.bfloat16)
    middle_update = panel_update(mid_adjoint, mid_panels, mid_valid)
    packed = jnp.concatenate([middle_update, carried], axis=2)
    mid_near = padded(packed, (("leaf", 0),), mid_count)
    width_split = middle_update.shape[2]
    to_top = route_blocks(
        mid_near[:, :, :width_split], near_mid_parents, near_mid_codes, own_top_nodes, 0
    )
    owner_hits = (near_mid_parents[None, :] == own_top_nodes[:, None]).astype(jnp.float32)
    to_top = to_top + jnp.einsum(
        "te,enw->tnw", owner_hits, mid_near[:, :, width_split:], precision=lax.Precision.HIGHEST
    )
    top_accum = top_cotangent.astype(jnp.float32) - to_top
    top_adjoint = solve_level(top_accum.astype(jnp.bfloat16), top_inverse).astype(jnp.bfloat16)
    leaf_rows = pick_rows(
        parent_ext, mid_near_ids, own_leaf_parents, own_leaf_codes, 0
    ) + pick_rows(grand_ext, top_far_ids, own_leaf_grand, own_leaf_codes, NB)
    leaf_rows = mask_columns(leaf_rows.astype(jnp.bfloat16), leaf_valid)
    mid_rows = pick_rows(grand_ext, top_far_ids, own_mid_parents, own_mid_codes, 0)
    mid_rows = mask_columns(mid_rows.astype(jnp.bfloat16), mid_valid)
    leaf_probes = lax.all_gather(leaf_adjoint, "rhs", axis=1, tiled=True)
    leaf_cols = lax.all_to_all(leaf_rows, "rhs", split_axis=2, concat_axis=1, tiled=True)
    leaf_grad = tile_grad(leaf_cols, leaf_probes)
    mid_probes = lax.all_gather(mid_adjoint, "rhs", axis=1, tiled=True)
    mid_cols = lax.all_to_all(mid_rows, "rhs", split_axis=2, concat_axis=1, tiled=True)
    mid_grad = tile_grad(mid_cols, mid_probes)
    return (
        leaf_adjoint,
        mid_adjoint,
        top_adjoint,
        leaf_grad.astype(jnp.bfloat16),
        mid_grad.astype(jnp.bfloat16),
    )


def solution(mesh):
    placed = (
        P(),
        P(),
        P(),
        P(),
        P("leaf"),
        P("leaf"),
        P("leaf", None, None),
        P("leaf", None, None),
        P("leaf", None, None),
        P("leaf", None, None),
        P("leaf", None, None),
        P("leaf", "rhs", None),
        P("leaf", "rhs", None),
        P("leaf", "rhs", None),
        P("leaf", "rhs", None),
        P("leaf", "rhs", None),
    )
    return jax.shard_map(
        shards,
        mesh=mesh,
        in_specs=placed,
        out_specs=(
            P("leaf", "rhs", None),
            P("leaf", "rhs", None),
            P("leaf", "rhs", None),
            P("leaf", "rhs", None),
            P("leaf", "rhs", None),
        ),
        check_vma=False,
    )
```

profile of v0, /device:TPU:0, one launch (start us, length us, event | category | flops | bytes accessed | tf_op | source)
XLA Modules:
  0.0 89.1 jit_solution(4280837738562392103)
XLA Ops:
  0.7 1.4 %collective-permute-start.8 = (bf16[1,32,512]{2,1,0:T(8,128)(2,1)}, bf16[1,32,512]{2,1,0:T(8,128)(2,1)S(1)}, u32[]{:S(2)}, u32[]{:S(2)}) collective-permute-start(bf16[1,32,512]{2,1,0:T(8,128)(2,1)} %param.31), channel_id=1, source_target_pairs={{4,0},{8,4},{12,8},{16,12},{20,16},{24,20},{28,24},{5,1},{9,5},{13... | collective-permute-start | bytes 98312 | tf_op jit(solution)/shard_map/ppermute | solution.py:27
  2.1 5.5 %collective-permute-start.7 = (bf16[1,32,512]{2,1,0:T(8,128)(2,1)}, bf16[1,32,512]{2,1,0:T(8,128)(2,1)S(1)}, u32[]{:S(2)}, u32[]{:S(2)}) collective-permute-start(bf16[1,32,512]{2,1,0:T(8,128)(2,1)} %param.31), channel_id=1, source_target_pairs={{0,4},{4,8},{8,12},{12,16},{16,20},{20,24},{24,28},{1,5},{5,9},{9,... | collective-permute-start | bytes 98312 | tf_op jit(solution)/shard_map/ppermute | solution.py:27
  7.6 4.0 %collective-permute-start.6 = (bf16[1,32,512]{2,1,0:T(8,128)(2,1)}, bf16[1,32,512]{2,1,0:T(8,128)(2,1)S(1)}, u32[]{:S(2)}, u32[]{:S(2)}) collective-permute-start(bf16[1,32,512]{2,1,0:T(8,128)(2,1)} %param.31), channel_id=1, source_target_pairs={{0,8},{4,12},{8,16},{12,20},{16,24},{20,28},{1,9},{5,13},{9,17},{1... | collective-permute-start | bytes 98312 | tf_op jit(solution)/shard_map/ppermute | solution.py:27
  11.6 1.3 %collective-permute-start.9 = (bf16[1,32,512]{2,1,0:T(8,128)(2,1)}, bf16[1,32,512]{2,1,0:T(8,128)(2,1)S(1)}, u32[]{:S(2)}, u32[]{:S(2)}) collective-permute-start(bf16[1,32,512]{2,1,0:T(8,128)(2,1)} %param.31), channel_id=1, source_target_pairs={{8,0},{12,4},{16,8},{20,12},{24,16},{28,20},{9,1},{13,5},{17,9},{2... | collective-permute-start | bytes 98312 | tf_op jit(solution)/shard_map/ppermute | solution.py:27
  12.9 5.0 %collective-permute-start.4 = (bf16[2,32,512]{2,1,0:T(8,128)(2,1)}, bf16[2,32,512]{2,1,0:T(8,128)(2,1)}, u32[]{:S(2)}, u32[]{:S(2)}) collective-permute-start(bf16[2,32,512]{2,1,0:T(8,128)(2,1)} %param.30), channel_id=1, source_target_pairs={{0,4},{4,8},{8,12},{12,16},{16,20},{20,24},{24,28},{1,5},{5,9},{9,... | collective-permute-start | bytes 196616 | tf_op jit(solution)/shard_map/ppermute | solution.py:16
  19.6 0.8 select_reduce_fusion.2
  20.5 0.8 select_reduce_fusion.1
  21.3 0.8 select_reduce_fusion
  25.3 0.9 %fusion.45 = s32[6]{0:T(128)S(1)} fusion(s32[6]{0:T(128)S(1)} %iota_add_fusion.1, s32[16]{0:T(128)} %bitcast.143), kind=kLoop, calls=%fused_computation.78 | loop fusion | flops 282 | bytes 112 | tf_op jit(solution)/shard_map/reduce_sum | solution.py:61
  28.0 1.0 %fusion.33 = s32[12]{0:T(128)S(1)} fusion(s32[12]{0:T(128)S(1)} %iota_add_fusion.3, s32[32]{0:T(128)} %bitcast.142), kind=kLoop, calls=%fused_computation.64 | loop fusion | flops 1140 | bytes 224 | tf_op jit(solution)/shard_map/reduce_sum | solution.py:61
  30.0 1.6 %convolution_convert_fusion = bf16[4,32,512]{2,1,0:T(8,128)(2,1)S(1)} fusion(bf16[4,32,512]{2,1,0:T(8,128)(2,1)} %param.27, bf16[4,512,512]{2,1,0:T(8,128)(2,1)S(1)} %copy-done), kind=kOutput, calls=%fused_computation.2 | convolution fusion | flops 67174400 | bytes 2359296 | tf_op jit(solution)/shard_map/dot_general | solution.py:31
  31.9 7.3 %all_gather.6 = bf16[4,128,512]{2,1,0:T(8,128)(2,1)S(1)} all-gather(bf16[4,32,512]{2,1,0:T(8,128)(2,1)S(1)} %convolution_convert_fusion), channel_id=1, replica_groups=mesh['leaf'=8,'rhs'=4] {'rhs'}, dimensions={1}, use_global_device_ids=true | all-gather | bytes 655360 | tf_op jit(solution)/shard_map/all_gather | solution.py:164
  39.2 1.3 %collective-permute-start.5 = (bf16[2,32,512]{2,1,0:T(8,128)(2,1)}, bf16[2,32,512]{2,1,0:T(8,128)(2,1)}, u32[]{:S(2)}, u32[]{:S(2)}) collective-permute-start(bf16[2,32,512]{2,1,0:T(8,128)(2,1)} %param.30), channel_id=1, source_target_pairs={{4,0},{8,4},{12,8},{16,12},{20,16},{24,20},{28,24},{5,1},{9,5},{13... | collective-permute-start | bytes 196616 | tf_op jit(solution)/shard_map/ppermute | solution.py:19
  40.6 1.3 %collective-permute-start.1 = (f32[4,32,128]{2,1,0:T(8,128)S(1)}, f32[4,32,128]{2,1,0:T(8,128)S(1)}, u32[]{:S(2)}, u32[]{:S(2)}) collective-permute-start(f32[4,32,128]{2,1,0:T(8,128)S(1)} %convolution_select_fusion), channel_id=1, source_target_pairs={{4,0},{8,4},{12,8},{16,12},{20,16},{24,20},{28,24},{5,1},{9,5},{13... | collective-permute-start | bytes 196616 | tf_op jit(solution)/shard_map/ppermute | solution.py:19
  41.9 5.2 %collective-permute-start = (f32[4,32,128]{2,1,0:T(8,128)S(1)}, f32[4,32,128]{2,1,0:T(8,128)S(1)}, u32[]{:S(2)}, u32[]{:S(2)}) collective-permute-start(f32[4,32,128]{2,1,0:T(8,128)S(1)} %convolution_select_fusion), channel_id=1, source_target_pairs={{0,4},{4,8},{8,12},{12,16},{16,20},{20,24},{24,28},{1,5},{5,9},{9,... | collective-permute-start | bytes 196616 | tf_op jit(solution)/shard_map/ppermute | solution.py:16
  48.4 3.3 %all-to-all-start.1 = ((bf16[4,2,1024]{2,1,0:T(2,128)(2,1)}), bf16[4,2,1024]{2,1,0:T(2,128)(2,1)S(1)}, u32[]{:S(2)}, u32[]{:S(2)}) async-start(bf16[4,2,1024]{2,1,0:T(2,128)(2,1)} %reshape.647), calls=%async_computation.1 | async-start | bytes 32768 | tf_op jit(solution)/shard_map/all_to_all | solution.py:168
  51.6 0.9 %convolution_bitcast_fusion.2 = f32[32,128,4]{1,2,0:T(4,128)} fusion(bf16[5,32,4,128]{3,2,1,0:T(4,128)(2,1)S(1)} %reshape.631, pred[4,4]{1,0:T(4,128)(4,1)S(1)} %get-tuple-element.12, pred[4,5]{0,1:T(8,128)(4,1)S(1)} %broadcast_compare_fusion.1), kind=kOutput, calls=%fused_computation.8 | convolution fusion | flops 655440 | bytes 229412 | tf_op jit(solution)/shard_map/smeb,enbc->snmc/dot_general | solution.py:90
  52.5 2.9 %all-to-all-done.1 = bf16[4,2,1024]{2,1,0:T(2,128)(2,1)S(1)} async-done(((bf16[4,2,1024]{2,1,0:T(2,128)(2,1)}), bf16[4,2,1024]{2,1,0:T(2,128)(2,1)S(1)}, u32[]{:S(2)}, u32[]{:S(2)}) %all-to-all-start.1) | async-done | bytes 16416 | tf_op jit(solution)/shard_map/all_to_all | solution.py:168
  56.9 1.6 %convolution_convert_fusion.1 = bf16[2,32,512]{2,1,0:T(8,128)(2,1)S(1)} fusion(bf16[2,512,512]{2,1,0:T(8,128)(2,1)} %param.23, f32[2,32,512]{2,0,1:T(2,128)S(1)} %reshape.625, bf16[2,32,512]{2,1,0:T(8,128)(2,1)S(1)} %copy-done.6), kind=kOutput, calls=%fused_computation.6 | convolution fusion | flops 33685504 | bytes 1310720 | tf_op jit(solution)/shard_map/dot_general | solution.py:31
  60.1 1.3 %collective-permute-start.3 = (f32[2,32,640]{2,0,1:T(2,128)}, f32[2,32,640]{2,0,1:T(2,128)}, u32[]{:S(2)}, u32[]{:S(2)}) collective-permute-start(f32[2,32,640]{2,0,1:T(2,128)} %constant_dynamic-update-slice_fusion), channel_id=1, source_target_pairs={{4,0},{8,4},{12,8},{16,12},{20,16},{24,20},{28,24},{5,1},{9,5},{13... | collective-permute-start | bytes 491528 | tf_op jit(solution)/shard_map/ppermute | solution.py:19
  61.4 6.1 %collective-permute-start.2 = (f32[2,32,640]{2,0,1:T(2,128)}, f32[2,32,640]{2,0,1:T(2,128)}, u32[]{:S(2)}, u32[]{:S(2)}) collective-permute-start(f32[2,32,640]{2,0,1:T(2,128)} %constant_dynamic-update-slice_fusion), channel_id=1, source_target_pairs={{0,4},{4,8},{8,12},{12,16},{16,20},{20,24},{24,28},{1,5},{5,9},{9,... | collective-permute-start | bytes 491528 | tf_op jit(solution)/shard_map/ppermute | solution.py:16
  67.5 5.8 %all_gather.7 = bf16[2,128,512]{2,1,0:T(8,128)(2,1)S(1)} all-gather(bf16[2,32,512]{2,1,0:T(8,128)(2,1)S(1)} %convolution_convert_fusion.1), channel_id=1, replica_groups=mesh['leaf'=8,'rhs'=4] {'rhs'}, dimensions={1}, use_global_device_ids=true | all-gather | bytes 327680 | tf_op jit(solution)/shard_map/all_gather | solution.py:167
  73.3 0.9 %pad_maximum_fusion.4 = bf16[6,32,512]{2,1,0:T(8,128)(2,1)S(1)} fusion(bf16[2,32,512]{2,1,0:T(8,128)(2,1)} %collective-permute-done.5, bf16[2,32,512]{2,1,0:T(8,128)(2,1)} %param.30, bf16[2,32,512]{2,1,0:T(8,128)(2,1)} %collective-permute-done.4), kind=kLoop, calls=%fused_computation.23 | loop fusion | flops 196608 | bytes 393216 | tf_op jit(solution)/shard_map/concatenate | solution.py:20
  74.3 1.0 %convolution_bitcast_fusion.3 = f32[32,128,4]{1,2,0:T(4,128)S(1)} fusion(bf16[6,32,4,128]{3,2,1,0:T(4,128)(2,1)S(1)} %reshape.630, pred[4,4]{1,0:T(4,128)(4,1)} %get-tuple-element.13, pred[4,6]{0,1:T(8,128)(4,1)} %broadcast_compare_fusion.2), kind=kOutput, calls=%fused_computation.9 | convolution fusion | flops 786528 | bytes 262184 | tf_op jit(solution)/shard_map/smeb,enbc->snmc/dot_general | solution.py:90
  75.2 0.9 fusion.21
  77.0 3.4 %all-to-all-start = ((bf16[4,2,2048]{2,1,0:T(2,128)(2,1)}), bf16[4,2,2048]{2,1,0:T(2,128)(2,1)S(1)}, u32[]{:S(2)}, u32[]{:S(2)}) async-start(bf16[4,2,2048]{2,1,0:T(2,128)(2,1)} %reshape.645), calls=%async_computation | async-start | bytes 65536 | tf_op jit(solution)/shard_map/all_to_all | solution.py:165
  80.4 0.8 fusion.1
  81.2 3.1 %all-to-all-done = bf16[4,2,2048]{2,1,0:T(2,128)(2,1)S(1)} async-done(((bf16[4,2,2048]{2,1,0:T(2,128)(2,1)}), bf16[4,2,2048]{2,1,0:T(2,128)(2,1)S(1)}, u32[]{:S(2)}, u32[]{:S(2)}) %all-to-all-start) | async-done | bytes 32800 | tf_op jit(solution)/shard_map/all_to_all | solution.py:165
  84.7 0.9 fusion
  85.6 1.6 %fusion.3 = f32[1,32,512]{2,0,1:T(1,128)S(1)} fusion(f32[2,32,640]{2,0,1:T(2,128)} %collective-permute-done.3, f32[2,32,640]{2,0,1:T(2,128)} %constant_dynamic-update-slice_fusion, f32[2,32,640]{2,0,1:T(2,128)} %collective-permute-done.2, pred[6]{0:T(512)(128)(4,1)} %select_compare_fusion), kind=kOutput, calls=%fused_computation.16 | convolution fusion | flops 1376256 | bytes 557062 | tf_op jit(solution)/shard_map/te,enw->tnw/dot_general | solution.py:153
  87.2 1.0 %fusion.8 = f32[32,128,4]{1,2,0:T(4,128)S(1)} fusion(f32[2,32,640]{2,0,1:T(2,128)} %collective-permute-done.3, f32[2,32,640]{2,0,1:T(2,128)} %constant_dynamic-update-slice_fusion, f32[2,32,640]{2,0,1:T(2,128)} %collective-permute-done.2, s32[6]{0:T(128)} %broadcast_select_fusion.1, pred[6]{0:T(512)(128)(4,1)} %select_compare_fusion), kind=kOutput, calls=%fused_computation.24 | convolution fusion | flops 1228848 | bytes 557086 | tf_op jit(solution)/shard_map/temb,enmc->tnbc/dot_general | solution.py:77
  88.2 0.9 fusion.2
  (86 shorter events, 13.4 us)
Async XLA Ops:
  0.6 29.4 %copy-start = (bf16[4,512,512]{2,1,0:T(8,128)(2,1)S(1)}, bf16[4,512,512]{2,1,0:T(8,128)(2,1)}, u32[]{:S(2)}) copy-start(bf16[4,512,512]{2,1,0:T(8,128)(2,1)} %param.22) | copy-start | bytes 6291460
  0.6 41.2 %copy-start.8 = (bf16[1,32,512]{2,1,0:T(8,128)(2,1)S(1)}, bf16[1,32,512]{2,1,0:T(8,128)(2,1)}, u32[]{:S(2)}) copy-start(bf16[1,32,512]{2,1,0:T(8,128)(2,1)} %param.31) | copy-start | bytes 98308
  0.7 31.0 %copy-start.3 = (bf16[4,128,512]{2,1,0:T(8,128)(2,1)S(1)}, bf16[4,128,512]{2,1,0:T(8,128)(2,1)}, u32[]{:S(2)}) copy-start(bf16[4,128,512]{2,1,0:T(8,128)(2,1)} %param.25) | copy-start | bytes 1572868
  0.7 41.2 %collective-permute-start.8 = (bf16[1,32,512]{2,1,0:T(8,128)(2,1)}, bf16[1,32,512]{2,1,0:T(8,128)(2,1)S(1)}, u32[]{:S(2)}, u32[]{:S(2)}) collective-permute-start(bf16[1,32,512]{2,1,0:T(8,128)(2,1)} %param.31), channel_id=1, source_target_pairs={{4,0},{8,4},{12,8},{16,12},{20,16},{24,20},{28,24},{5,1},{9,5},{13... | collective-permute-start | bytes 98312 | tf_op jit(solution)/shard_map/ppermute | solution.py:27
  2.1 38.5 %collective-permute-start.7 = (bf16[1,32,512]{2,1,0:T(8,128)(2,1)}, bf16[1,32,512]{2,1,0:T(8,128)(2,1)S(1)}, u32[]{:S(2)}, u32[]{:S(2)}) collective-permute-start(bf16[1,32,512]{2,1,0:T(8,128)(2,1)} %param.31), channel_id=1, source_target_pairs={{0,4},{4,8},{8,12},{12,16},{16,20},{20,24},{24,28},{1,5},{5,9},{9,... | collective-permute-start | bytes 98312 | tf_op jit(solution)/shard_map/ppermute | solution.py:27
  7.6 31.6 %collective-permute-start.6 = (bf16[1,32,512]{2,1,0:T(8,128)(2,1)}, bf16[1,32,512]{2,1,0:T(8,128)(2,1)S(1)}, u32[]{:S(2)}, u32[]{:S(2)}) collective-permute-start(bf16[1,32,512]{2,1,0:T(8,128)(2,1)} %param.31), channel_id=1, source_target_pairs={{0,8},{4,12},{8,16},{12,20},{16,24},{20,28},{1,9},{5,13},{9,17},{1... | collective-permute-start | bytes 98312 | tf_op jit(solution)/shard_map/ppermute | solution.py:27
  11.6 35.5 %collective-permute-start.9 = (bf16[1,32,512]{2,1,0:T(8,128)(2,1)}, bf16[1,32,512]{2,1,0:T(8,128)(2,1)S(1)}, u32[]{:S(2)}, u32[]{:S(2)}) collective-permute-start(bf16[1,32,512]{2,1,0:T(8,128)(2,1)} %param.31), channel_id=1, source_target_pairs={{8,0},{12,4},{16,8},{20,12},{24,16},{28,20},{9,1},{13,5},{17,9},{2... | collective-permute-start | bytes 98312 | tf_op jit(solution)/shard_map/ppermute | solution.py:27
  12.9 60.3 %collective-permute-start.4 = (bf16[2,32,512]{2,1,0:T(8,128)(2,1)}, bf16[2,32,512]{2,1,0:T(8,128)(2,1)}, u32[]{:S(2)}, u32[]{:S(2)}) collective-permute-start(bf16[2,32,512]{2,1,0:T(8,128)(2,1)} %param.30), channel_id=1, source_target_pairs={{0,4},{4,8},{8,12},{12,16},{16,20},{20,24},{24,28},{1,5},{5,9},{9,... | collective-permute-start | bytes 196616 | tf_op jit(solution)/shard_map/ppermute | solution.py:16
  23.1 8.6 %copy-start.9 = (pred[4,128]{1,0:T(4,128)(4,1)}, pred[4,128]{1,0:T(4,128)(4,1)S(1)}, u32[]{:S(2)}) copy-start(pred[4,128]{1,0:T(4,128)(4,1)S(1)} %iota_compare_fusion.8) | copy-start | bytes 1540
  23.8 23.7 %copy-start.10 = (pred[2,128]{1,0:T(4,128)(4,1)}, pred[2,128]{1,0:T(4,128)(4,1)S(1)}, u32[]{:S(2)}) copy-start(pred[2,128]{1,0:T(4,128)(4,1)S(1)} %iota_compare_fusion.10) | copy-start | bytes 772
  31.7 25.0 %copy-start.1 = (bf16[4,32,512]{2,1,0:T(8,128)(2,1)}, bf16[4,32,512]{2,1,0:T(8,128)(2,1)S(1)}, u32[]{:S(2)}) copy-start(bf16[4,32,512]{2,1,0:T(8,128)(2,1)S(1)} %convolution_convert_fusion) | copy-start | bytes 393220
  31.9 24.9 %copy-start.6 = (bf16[2,32,512]{2,1,0:T(8,128)(2,1)S(1)}, bf16[2,32,512]{2,1,0:T(8,128)(2,1)}, u32[]{:S(2)}) copy-start(bf16[2,32,512]{2,1,0:T(8,128)(2,1)} %param.28) | copy-start | bytes 196612
  39.2 34.0 %collective-permute-start.5 = (bf16[2,32,512]{2,1,0:T(8,128)(2,1)}, bf16[2,32,512]{2,1,0:T(8,128)(2,1)}, u32[]{:S(2)}, u32[]{:S(2)}) collective-permute-start(bf16[2,32,512]{2,1,0:T(8,128)(2,1)} %param.30), channel_id=1, source_target_pairs={{4,0},{8,4},{12,8},{16,12},{20,16},{24,20},{28,24},{5,1},{9,5},{13... | collective-permute-start | bytes 196616 | tf_op jit(solution)/shard_map/ppermute | solution.py:19
  40.6 15.2 %collective-permute-start.1 = (f32[4,32,128]{2,1,0:T(8,128)S(1)}, f32[4,32,128]{2,1,0:T(8,128)S(1)}, u32[]{:S(2)}, u32[]{:S(2)}) collective-permute-start(f32[4,32,128]{2,1,0:T(8,128)S(1)} %convolution_select_fusion), channel_id=1, source_target_pairs={{4,0},{8,4},{12,8},{16,12},{20,16},{24,20},{28,24},{5,1},{9,5},{13... | collective-permute-start | bytes 196616 | tf_op jit(solution)/shard_map/ppermute | solution.py:19
  41.9 13.8 %collective-permute-start = (f32[4,32,128]{2,1,0:T(8,128)S(1)}, f32[4,32,128]{2,1,0:T(8,128)S(1)}, u32[]{:S(2)}, u32[]{:S(2)}) collective-permute-start(f32[4,32,128]{2,1,0:T(8,128)S(1)} %convolution_select_fusion), channel_id=1, source_target_pairs={{0,4},{4,8},{8,12},{12,16},{16,20},{20,24},{24,28},{1,5},{5,9},{9,... | collective-permute-start | bytes 196616 | tf_op jit(solution)/shard_map/ppermute | solution.py:16
  47.2 11.3 %copy-start.5 = (bf16[2,128,512]{2,1,0:T(8,128)(2,1)S(1)}, bf16[2,128,512]{2,1,0:T(8,128)(2,1)}, u32[]{:S(2)}) copy-start(bf16[2,128,512]{2,1,0:T(8,128)(2,1)} %param.26) | copy-start | bytes 786436
  48.4 7.1 %all-to-all-start.1 = ((bf16[4,2,1024]{2,1,0:T(2,128)(2,1)}), bf16[4,2,1024]{2,1,0:T(2,128)(2,1)S(1)}, u32[]{:S(2)}, u32[]{:S(2)}) async-start(bf16[4,2,1024]{2,1,0:T(2,128)(2,1)} %reshape.647), calls=%async_computation.1 | async-start | bytes 32768 | tf_op jit(solution)/shard_map/all_to_all | solution.py:168
  55.8 2.8 %copy-start.11 = (pred[2,128]{1,0:T(4,128)(4,1)S(1)}, pred[2,128]{1,0:T(4,128)(4,1)}, u32[]{:S(2)}) copy-start(pred[2,128]{1,0:T(4,128)(4,1)} %copy-done.10) | copy-start | bytes 772
  58.5 27.1 %copy-start.2 = (bf16[2,32,512]{2,1,0:T(8,128)(2,1)}, bf16[2,32,512]{2,1,0:T(8,128)(2,1)S(1)}, u32[]{:S(2)}) copy-start(bf16[2,32,512]{2,1,0:T(8,128)(2,1)S(1)} %convolution_convert_fusion.1) | copy-start | bytes 196612
  60.1 25.5 %collective-permute-start.3 = (f32[2,32,640]{2,0,1:T(2,128)}, f32[2,32,640]{2,0,1:T(2,128)}, u32[]{:S(2)}, u32[]{:S(2)}) collective-permute-start(f32[2,32,640]{2,0,1:T(2,128)} %constant_dynamic-update-slice_fusion), channel_id=1, source_target_pairs={{4,0},{8,4},{12,8},{16,12},{20,16},{24,20},{28,24},{5,1},{9,5},{13... | collective-permute-start | bytes 491528 | tf_op jit(solution)/shard_map/ppermute | solution.py:19
  61.4 24.2 %collective-permute-start.2 = (f32[2,32,640]{2,0,1:T(2,128)}, f32[2,32,640]{2,0,1:T(2,128)}, u32[]{:S(2)}, u32[]{:S(2)}) collective-permute-start(f32[2,32,640]{2,0,1:T(2,128)} %constant_dynamic-update-slice_fusion), channel_id=1, source_target_pairs={{0,4},{4,8},{8,12},{12,16},{16,20},{20,24},{24,28},{1,5},{5,9},{9,... | collective-permute-start | bytes 491528 | tf_op jit(solution)/shard_map/ppermute | solution.py:16
  74.2 14.0 %copy-start.7 = (bf16[1,32,512]{2,1,0:T(8,128)(2,1)S(1)}, bf16[1,32,512]{2,1,0:T(8,128)(2,1)}, u32[]{:S(2)}) copy-start(bf16[1,32,512]{2,1,0:T(8,128)(2,1)} %param.29) | copy-start | bytes 98308
  77.0 11.2 %copy-start.4 = (bf16[1,512,512]{2,1,0:T(8,128)(2,1)S(1)}, bf16[1,512,512]{2,1,0:T(8,128)(2,1)}, u32[]{:S(2)}) copy-start(bf16[1,512,512]{2,1,0:T(8,128)(2,1)} %param.24) | copy-start | bytes 1572868
  77.0 7.3 %all-to-all-start = ((bf16[4,2,2048]{2,1,0:T(2,128)(2,1)}), bf16[4,2,2048]{2,1,0:T(2,128)(2,1)S(1)}, u32[]{:S(2)}, u32[]{:S(2)}) async-start(bf16[4,2,2048]{2,1,0:T(2,128)(2,1)} %reshape.645), calls=%async_computation | async-start | bytes 65536 | tf_op jit(solution)/shard_map/all_to_all | solution.py:165
where the time goes:
time: 90.1 us; the launch traced here: 89.1 us
  starting transfers between devices  39 us (43%)
  blocking collectives  13.1 us (15%)
  matrix products  11.8 us (13%)
  other arithmetic  11.7 us (13%)
  local copies, waits for them, and re-layouts  6.33 us (7%)
  waiting for transfers between devices  6.04 us (7%)
  between operations  1.1 us (1%)
    ppermute x3, starting transfers between devices, padded(): lax.ppermute(lax.slice_in_dim(block, block.shape[dim] - width, None, axis...  16.3 us
    ppermute x4, starting transfers between devices, from_behind(): return lax.ppermute(value, axis, pairs)  12.2 us
    all_gather x1, blocking collectives, shards(): leaf_probes = lax.all_gather(leaf_adjoint, 'rhs', axis=1, tiled=True)  7.31 us
    all_gather x1, blocking collectives, shards(): mid_probes = lax.all_gather(mid_adjoint, 'rhs', axis=1, tiled=True)  5.76 us
    reduce_sum x5, other arithmetic, table_pick(): values = jnp.sum(jnp.where(spread_match, table[None], 0), axis=1)  4.45 us
    dot_general x3, matrix products, solve_level(): lax.dot_general(block_rows, inverse, (((2,), (2,)), ((0,), (0,))), prefer...  4.12 us
    ppermute x3, starting transfers between devices, padded(): lax.ppermute(lax.slice_in_dim(block, 0, width, axis=dim), axis, backward)  3.85 us
    all_to_all x1, starting transfers between devices, shards(): lax.all_to_all(leaf_rows, 'rhs', split_axis=2, concat_axis=1, tiled=True)  3.4 us
  transfers between devices with their start and end apart: 12, of which 2 were waited for; matrix products, arithmetic and copies ran while one was open for 29% of the time, Pallas kernels for 0%

commit v1 on v0

--- a/solution.py
+++ b/solution.py
@@ -2,6 +2,7 @@
 import jax.numpy as jnp
 from jax import lax
 from jax.sharding import PartitionSpec as P
+from jax.lax import axis_index, axis_size, ppermute
 
 BLK = 128
 MR = 128
@@ -161,7 +162,19 @@
     leaf_rows = mask_columns(leaf_rows.astype(jnp.bfloat16), leaf_valid)
     mid_rows = pick_rows(grand_ext, top_far_ids, own_mid_parents, own_mid_codes, 0)
     mid_rows = mask_columns(mid_rows.astype(jnp.bfloat16), mid_valid)
-    leaf_probes = lax.all_gather(leaf_adjoint, "rhs", axis=1, tiled=True)
+    num_devices = axis_size("rhs")
+    panels = tuple(((to_i, (to_i + 1) % num_devices) for to_i in range(num_devices)))
+    samples = tuple(((to_i, (to_i - 1) % num_devices) for to_i in range(num_devices)))
+    e_now, passed = ([leaf_adjoint], [leaf_adjoint])
+    for _ in range(num_devices // 2):
+        e_now.append(ppermute(e_now[-1], perm=panels, axis_name="rhs"))
+    for _ in range((num_devices - 1) // 2):
+        passed.append(ppermute(passed[-1], axis_name="rhs", perm=samples))
+    leaf_probes = jnp.roll(
+        jnp.concatenate([*e_now[::-1], *passed[1:]], axis=1),
+        (axis_index("rhs") - num_devices // 2) * leaf_adjoint.shape[1],
+        axis=1,
+    )
     leaf_cols = lax.all_to_all(leaf_rows, "rhs", split_axis=2, concat_axis=1, tiled=True)
     leaf_grad = tile_grad(leaf_cols, leaf_probes)
     mid_probes = lax.all_gather(mid_adjoint, "rhs", axis=1, tiled=True)

time: 90.1 us -> 95.4 us (1.059)
  local copies, waits for them, and re-layouts: 6.33 us -> 15.1 us
  blocking collectives: 13.1 us -> 5.89 us
  matrix products: 11.8 us -> 14.1 us
  other arithmetic: 11.7 us -> 12.9 us
    all_gather x1 -> x0, blocking collectives: 7.31 us -> none  [shards(): leaf_probes = lax.all_gather(leaf_adjoint, 'rhs', axis=1, tiled=True)]
    unnamed x33 -> x46, local copies, waits for them, and re-layouts: 2.53 us -> 8.12 us
    ppermute x0 -> x3, waiting for transfers between devices: none -> 1.04 us  [the longest x2 1.04 us: shards(): e_now.append(ppermute(e_now[-1], perm=panels, axis_name='rhs'))]
    dot_general x2, matrix products: 0.43 us -> 1.43 us  [panel_update(): lax.dot_general(adjoint_rows, panel_block, (((2,), (2,)), ((0,), (0,))),...]
  transfers between devices with their start and end apart: 12 -> 15, of which waited for: 2 -> 3; matrix products, arithmetic and copies ran while one was open for 29% -> 40% of each run, Pallas kernels for 0% -> 0%
where the time goes in v1:
time: 95.4 us; the launch traced here: 94.3 us
  starting transfers between devices  39.1 us (41%)
  local copies, waits for them, and re-layouts  15.1 us (16%)
  matrix products  14.1 us (15%)
  other arithmetic  12.9 us (14%)
  waiting for transfers between devices  6.17 us (6%)
  blocking collectives  5.89 us (6%)
  between operations  1.14 us (1%)
    ppermute x3, starting transfers between devices, padded(): lax.ppermute(lax.slice_in_dim(block, block.shape[dim] - width, None, axis...  16.2 us
    ppermute x4, starting transfers between devices, from_behind(): return lax.ppermute(value, axis, pairs)  12.2 us
    unnamed x46, local copies, waits for them, and re-layouts  8.12 us
    all_gather x1, blocking collectives, shards(): mid_probes = lax.all_gather(mid_adjoint, 'rhs', axis=1, tiled=True)  5.89 us
    reduce_sum x5, other arithmetic, table_pick(): values = jnp.sum(jnp.where(spread_match, table[None], 0), axis=1)  4.45 us
    ppermute x3, starting transfers between devices, padded(): lax.ppermute(lax.slice_in_dim(block, 0, width, axis=dim), axis, backward)  4 us
    dot_general x3, matrix products, solve_level(): lax.dot_general(block_rows, inverse, (((2,), (2,)), ((0,), (0,))), prefer...  3.8 us
    all_to_all x1, starting transfers between devices, shards(): lax.all_to_all(leaf_rows, 'rhs', split_axis=2, concat_axis=1, tiled=True)  3.26 us
  transfers between devices with their start and end apart: 15, of which 3 were waited for; matrix products, arithmetic and copies ran while one was open for 40% of the time, Pallas kernels for 0%

profile of v1, /device:TPU:0, one launch (start us, length us, event | category | flops | bytes accessed | tf_op | source)
XLA Modules:
  0.0 94.3 jit_solution(12527298000870740796)
XLA Ops:
  0.7 1.4 %collective-permute-start.8 = (bf16[1,32,512]{2,1,0:T(8,128)(2,1)}, bf16[1,32,512]{2,1,0:T(8,128)(2,1)S(1)}, u32[]{:S(2)}, u32[]{:S(2)}) collective-permute-start(bf16[1,32,512]{2,1,0:T(8,128)(2,1)} %param.31), channel_id=1, source_target_pairs={{4,0},{8,4},{12,8},{16,12},{20,16},{24,20},{28,24},{5,1},{9,5},{13... | collective-permute-start | bytes 98312 | tf_op jit(solution)/shard_map/ppermute | solution.py:28
  2.1 5.5 %collective-permute-start.7 = (bf16[1,32,512]{2,1,0:T(8,128)(2,1)}, bf16[1,32,512]{2,1,0:T(8,128)(2,1)S(1)}, u32[]{:S(2)}, u32[]{:S(2)}) collective-permute-start(bf16[1,32,512]{2,1,0:T(8,128)(2,1)} %param.31), channel_id=1, source_target_pairs={{0,4},{4,8},{8,12},{12,16},{16,20},{20,24},{24,28},{1,5},{5,9},{9,... | collective-permute-start | bytes 98312 | tf_op jit(solution)/shard_map/ppermute | solution.py:28
  7.6 4.0 %collective-permute-start.6 = (bf16[1,32,512]{2,1,0:T(8,128)(2,1)}, bf16[1,32,512]{2,1,0:T(8,128)(2,1)S(1)}, u32[]{:S(2)}, u32[]{:S(2)}) collective-permute-start(bf16[1,32,512]{2,1,0:T(8,128)(2,1)} %param.31), channel_id=1, source_target_pairs={{0,8},{4,12},{8,16},{12,20},{16,24},{20,28},{1,9},{5,13},{9,17},{1... | collective-permute-start | bytes 98312 | tf_op jit(solution)/shard_map/ppermute | solution.py:28
  11.6 1.3 %collective-permute-start.9 = (bf16[1,32,512]{2,1,0:T(8,128)(2,1)}, bf16[1,32,512]{2,1,0:T(8,128)(2,1)S(1)}, u32[]{:S(2)}, u32[]{:S(2)}) collective-permute-start(bf16[1,32,512]{2,1,0:T(8,128)(2,1)} %param.31), channel_id=1, source_target_pairs={{8,0},{12,4},{16,8},{20,12},{24,16},{28,20},{9,1},{13,5},{17,9},{2... | collective-permute-start | bytes 98312 | tf_op jit(solution)/shard_map/ppermute | solution.py:28
  12.9 5.0 %collective-permute-start.4 = (bf16[2,32,512]{2,1,0:T(8,128)(2,1)}, bf16[2,32,512]{2,1,0:T(8,128)(2,1)}, u32[]{:S(2)}, u32[]{:S(2)}) collective-permute-start(bf16[2,32,512]{2,1,0:T(8,128)(2,1)} %param.30), channel_id=1, source_target_pairs={{0,4},{4,8},{8,12},{12,16},{16,20},{20,24},{24,28},{1,5},{5,9},{9,... | collective-permute-start | bytes 196616 | tf_op jit(solution)/shard_map/ppermute | solution.py:17
  25.3 0.9 fusion.46
  28.1 1.0 %fusion.34 = s32[12]{0:T(128)S(1)} fusion(s32[12]{0:T(128)S(1)} %iota_add_fusion.3, s32[32]{0:T(128)} %bitcast.141), kind=kLoop, calls=%fused_computation.73 | loop fusion | flops 1140 | bytes 224 | tf_op jit(solution)/shard_map/reduce_sum | solution.py:62
  30.5 1.6 %convolution_convert_fusion = bf16[4,32,512]{2,1,0:T(8,128)(2,1)S(1)} fusion(bf16[4,32,512]{2,1,0:T(8,128)(2,1)} %param.27, bf16[4,512,512]{2,1,0:T(8,128)(2,1)S(1)} %copy-done), kind=kOutput, calls=%fused_computation.2 | convolution fusion | flops 67174400 | bytes 2359296 | tf_op jit(solution)/shard_map/dot_general | solution.py:32
  32.5 1.3 %collective-permute-start.5 = (bf16[2,32,512]{2,1,0:T(8,128)(2,1)}, bf16[2,32,512]{2,1,0:T(8,128)(2,1)}, u32[]{:S(2)}, u32[]{:S(2)}) collective-permute-start(bf16[2,32,512]{2,1,0:T(8,128)(2,1)} %param.30), channel_id=1, source_target_pairs={{4,0},{8,4},{12,8},{16,12},{20,16},{24,20},{28,24},{5,1},{9,5},{13... | collective-permute-start | bytes 196616 | tf_op jit(solution)/shard_map/ppermute | solution.py:20
  34.5 1.3 %collective-permute-start.1 = (f32[4,32,128]{2,1,0:T(8,128)S(1)}, f32[4,32,128]{2,1,0:T(8,128)}, u32[]{:S(2)}, u32[]{:S(2)}) collective-permute-start(f32[4,32,128]{2,1,0:T(8,128)S(1)} %convolution_select_fusion), channel_id=1, source_target_pairs={{4,0},{8,4},{12,8},{16,12},{20,16},{24,20},{28,24},{5,1},{9,5},{13... | collective-permute-start | bytes 196616 | tf_op jit(solution)/shard_map/ppermute | solution.py:20
  37.0 5.8 %collective-permute-start = (f32[4,32,128]{2,1,0:T(8,128)S(1)}, f32[4,32,128]{2,1,0:T(8,128)}, u32[]{:S(2)}, u32[]{:S(2)}) collective-permute-start(f32[4,32,128]{2,1,0:T(8,128)S(1)} %convolution_select_fusion), channel_id=1, source_target_pairs={{0,4},{4,8},{8,12},{12,16},{16,20},{20,24},{24,28},{1,5},{5,9},{9,... | collective-permute-start | bytes 196616 | tf_op jit(solution)/shard_map/ppermute | solution.py:17
  44.0 1.0 %reshape.631 = bf16[5,32,4,128]{3,2,1,0:T(4,128)(2,1)S(1)} reshape(bf16[5,32,512]{2,1,0:T(8,128)(2,1)} %constant_dynamic-update-slice_fusion.2) | data formatting | bytes 327680 | tf_op jit(solution)/shard_map/reshape | solution.py:90
  46.5 3.3 %all-to-all-start.1 = ((bf16[4,2,1024]{2,1,0:T(2,128)(2,1)}), bf16[4,2,1024]{2,1,0:T(2,128)(2,1)S(1)}, u32[]{:S(2)}, u32[]{:S(2)}) async-start(bf16[4,2,1024]{2,1,0:T(2,128)(2,1)} %reshape.647), calls=%async_computation.1 | async-start | bytes 32768 | tf_op jit(solution)/shard_map/all_to_all | solution.py:181
  49.8 1.8 %convolution_bitcast_fusion.2 = f32[32,128,4]{1,2,0:T(4,128)} fusion(bf16[5,32,4,128]{3,2,1,0:T(4,128)(2,1)} %copy-done.6, pred[4,4]{1,0:T(4,128)(4,1)S(1)} %get-tuple-element.12, pred[4,5]{0,1:T(8,128)(4,1)S(1)} %broadcast_compare_fusion.1), kind=kOutput, calls=%fused_computation.8 | convolution fusion | flops 655440 | bytes 229412 | tf_op jit(solution)/shard_map/smeb,enbc->snmc/dot_general | solution.py:91
  51.6 2.0 %all-to-all-done.1 = bf16[4,2,1024]{2,1,0:T(2,128)(2,1)S(1)} async-done(((bf16[4,2,1024]{2,1,0:T(2,128)(2,1)}), bf16[4,2,1024]{2,1,0:T(2,128)(2,1)S(1)}, u32[]{:S(2)}, u32[]{:S(2)}) %all-to-all-start.1) | async-done | bytes 16416 | tf_op jit(solution)/shard_map/all_to_all | solution.py:181
  55.3 1.1 %convolution_bitcast_fusion.1 = f32[2,32,4,128]{3,2,0,1:T(4,128)S(1)} fusion(f32[12,32,128,1]{2,1,0,3:T(8,128)S(1)} %maximum_bitcast_fusion, pred[12,4]{0,1:T(4,128)(4,1)} %get-tuple-element.11, pred[2,12]{1,0:T(4,128)(4,1)} %copy-done.12), kind=kOutput, calls=%fused_computation.5 | convolution fusion | flops 4718688 | bytes 327752 | tf_op jit(solution)/shard_map/temb,enmc->tnbc/dot_general | solution.py:78
  57.3 1.3 %convolution_convert_fusion.1 = bf16[2,32,512]{2,1,0:T(8,128)(2,1)S(1)} fusion(bf16[2,512,512]{2,1,0:T(8,128)(2,1)S(1)} %copy-done.2, f32[2,32,512]{2,0,1:T(2,128)} %reshape.625, bf16[2,32,512]{2,1,0:T(8,128)(2,1)} %param.28), kind=kOutput, calls=%fused_computation.6 | convolution fusion | flops 33685504 | bytes 1310720 | tf_op jit(solution)/shard_map/dot_general | solution.py:32
  58.6 1.2 %convolution_select_fusion.1 = f32[2,32,128]{2,1,0:T(8,128)S(1)} fusion(bf16[2,32,512]{2,1,0:T(8,128)(2,1)S(1)} %convolution_convert_fusion.1, bf16[2,128,512]{2,1,0:T(8,128)(2,1)} %param.26, pred[2,128]{1,0:T(4,128)(4,1)} %copy-done.11), kind=kOutput, calls=%fused_computation.14 | convolution fusion | flops 8396800 | bytes 360704 | tf_op jit(solution)/shard_map/dot_general | solution.py:45
  61.1 1.4 %collective-permute-start.3 = (f32[2,32,640]{2,0,1:T(2,128)}, f32[2,32,640]{2,0,1:T(2,128)}, u32[]{:S(2)}, u32[]{:S(2)}) collective-permute-start(f32[2,32,640]{2,0,1:T(2,128)} %constant_dynamic-update-slice_fusion), channel_id=1, source_target_pairs={{4,0},{8,4},{12,8},{16,12},{20,16},{24,20},{28,24},{5,1},{9,5},{13... | collective-permute-start | bytes 491528 | tf_op jit(solution)/shard_map/ppermute | solution.py:20
  62.5 5.9 %all_gather.3 = bf16[2,128,512]{2,1,0:T(8,128)(2,1)S(1)} all-gather(bf16[2,32,512]{2,1,0:T(8,128)(2,1)S(1)} %convolution_convert_fusion.1), channel_id=1, replica_groups=mesh['leaf'=8,'rhs'=4] {'rhs'}, dimensions={1}, use_global_device_ids=true | all-gather | bytes 327680 | tf_op jit(solution)/shard_map/all_gather | solution.py:180
  68.4 5.5 %collective-permute-start.2 = (f32[2,32,640]{2,0,1:T(2,128)}, f32[2,32,640]{2,0,1:T(2,128)}, u32[]{:S(2)}, u32[]{:S(2)}) collective-permute-start(f32[2,32,640]{2,0,1:T(2,128)} %constant_dynamic-update-slice_fusion), channel_id=1, source_target_pairs={{0,4},{4,8},{8,12},{12,16},{16,20},{20,24},{24,28},{1,5},{5,9},{9,... | collective-permute-start | bytes 491528 | tf_op jit(solution)/shard_map/ppermute | solution.py:17
  73.9 0.9 pad_maximum_fusion.4
  75.0 1.0 %convolution_bitcast_fusion.3 = f32[32,128,4]{1,2,0:T(4,128)S(1)} fusion(bf16[6,32,4,128]{3,2,1,0:T(4,128)(2,1)S(1)} %reshape.630, pred[4,4]{1,0:T(4,128)(4,1)} %get-tuple-element.13, pred[4,6]{0,1:T(8,128)(4,1)} %broadcast_compare_fusion.2), kind=kOutput, calls=%fused_computation.9 | convolution fusion | flops 786528 | bytes 262184 | tf_op jit(solution)/shard_map/smeb,enbc->snmc/dot_general | solution.py:91
  77.4 3.3 %all-to-all-start = ((bf16[4,2,2048]{2,1,0:T(2,128)(2,1)}), bf16[4,2,2048]{2,1,0:T(2,128)(2,1)S(1)}, u32[]{:S(2)}, u32[]{:S(2)}) async-start(bf16[4,2,2048]{2,1,0:T(2,128)(2,1)} %reshape.645), calls=%async_computation | async-start | bytes 65536 | tf_op jit(solution)/shard_map/all_to_all | solution.py:178
  81.5 3.1 %all-to-all-done = bf16[4,2,2048]{2,1,0:T(2,128)(2,1)S(1)} async-done(((bf16[4,2,2048]{2,1,0:T(2,128)(2,1)}), bf16[4,2,2048]{2,1,0:T(2,128)(2,1)S(1)}, u32[]{:S(2)}, u32[]{:S(2)}) %all-to-all-start) | async-done | bytes 32800 | tf_op jit(solution)/shard_map/all_to_all | solution.py:178
  85.1 1.6 %fusion.3 = f32[1,32,512]{2,0,1:T(1,128)S(1)} fusion(f32[2,32,640]{2,0,1:T(2,128)} %collective-permute-done.3, f32[2,32,640]{2,0,1:T(2,128)} %constant_dynamic-update-slice_fusion, f32[2,32,640]{2,0,1:T(2,128)} %collective-permute-done.2, pred[6]{0:T(512)(128)(4,1)} %select_compare_fusion), kind=kOutput, calls=%fused_computation.16 | convolution fusion | flops 1376256 | bytes 557062 | tf_op jit(solution)/shard_map/te,enw->tnw/dot_general | solution.py:154
  86.7 1.0 %fusion.9 = f32[32,128,4]{1,2,0:T(4,128)S(1)} fusion(f32[2,32,640]{2,0,1:T(2,128)} %collective-permute-done.3, f32[2,32,640]{2,0,1:T(2,128)} %constant_dynamic-update-slice_fusion, f32[2,32,640]{2,0,1:T(2,128)} %collective-permute-done.2, s32[6]{0:T(128)S(1)} %copy-done.14, pred[6]{0:T(512)(128)(4,1)S(1)} %copy-done.13), kind=kOutput, calls=%fused_computation.25 | convolution fusion | flops 1228848 | bytes 557086 | tf_op jit(solution)/shard_map/temb,enmc->tnbc/dot_general | solution.py:78
  88.6 1.0 %collective-permute-done.11 = bf16[4,32,512]{2,1,0:T(8,128)(2,1)S(1)} collective-permute-done((bf16[4,32,512]{2,1,0:T(8,128)(2,1)}, bf16[4,32,512]{2,1,0:T(8,128)(2,1)S(1)}, u32[]{:S(2)}, u32[]{:S(2)}) %collective-permute-start.11) | collective-permute-done | bytes 131104 | tf_op jit(solution)/shard_map/ppermute | solution.py:170
  89.7 0.9 constant_dynamic-update-slice_fusion.13
  90.6 0.9 constant_dynamic-update-slice_fusion.11
  91.6 0.9 constant_dynamic-update-slice_fusion.9
  92.5 0.9 constant_dynamic-update-slice_fusion.7
  (105 shorter events, 24.1 us)
Async XLA Ops:
  0.6 29.9 %copy-start = (bf16[4,512,512]{2,1,0:T(8,128)(2,1)S(1)}, bf16[4,512,512]{2,1,0:T(8,128)(2,1)}, u32[]{:S(2)}) copy-start(bf16[4,512,512]{2,1,0:T(8,128)(2,1)} %param.22) | copy-start | bytes 6291460
  0.6 35.7 %copy-start.9 = (bf16[1,32,512]{2,1,0:T(8,128)(2,1)S(1)}, bf16[1,32,512]{2,1,0:T(8,128)(2,1)}, u32[]{:S(2)}) copy-start(bf16[1,32,512]{2,1,0:T(8,128)(2,1)} %param.31) | copy-start | bytes 98308
  0.7 36.3 %collective-permute-start.8 = (bf16[1,32,512]{2,1,0:T(8,128)(2,1)}, bf16[1,32,512]{2,1,0:T(8,128)(2,1)S(1)}, u32[]{:S(2)}, u32[]{:S(2)}) collective-permute-start(bf16[1,32,512]{2,1,0:T(8,128)(2,1)} %param.31), channel_id=1, source_target_pairs={{4,0},{8,4},{12,8},{16,12},{20,16},{24,20},{28,24},{5,1},{9,5},{13... | collective-permute-start | bytes 98312 | tf_op jit(solution)/shard_map/ppermute | solution.py:28
  2.1 32.4 %collective-permute-start.7 = (bf16[1,32,512]{2,1,0:T(8,128)(2,1)}, bf16[1,32,512]{2,1,0:T(8,128)(2,1)S(1)}, u32[]{:S(2)}, u32[]{:S(2)}) collective-permute-start(bf16[1,32,512]{2,1,0:T(8,128)(2,1)} %param.31), channel_id=1, source_target_pairs={{0,4},{4,8},{8,12},{12,16},{16,20},{20,24},{24,28},{1,5},{5,9},{9,... | collective-permute-start | bytes 98312 | tf_op jit(solution)/shard_map/ppermute | solution.py:28
  7.6 24.9 %collective-permute-start.6 = (bf16[1,32,512]{2,1,0:T(8,128)(2,1)}, bf16[1,32,512]{2,1,0:T(8,128)(2,1)S(1)}, u32[]{:S(2)}, u32[]{:S(2)}) collective-permute-start(bf16[1,32,512]{2,1,0:T(8,128)(2,1)} %param.31), channel_id=1, source_target_pairs={{0,8},{4,12},{8,16},{12,20},{16,24},{20,28},{1,9},{5,13},{9,17},{1... | collective-permute-start | bytes 98312 | tf_op jit(solution)/shard_map/ppermute | solution.py:28
  11.6 31.8 %collective-permute-start.9 = (bf16[1,32,512]{2,1,0:T(8,128)(2,1)}, bf16[1,32,512]{2,1,0:T(8,128)(2,1)S(1)}, u32[]{:S(2)}, u32[]{:S(2)}) collective-permute-start(bf16[1,32,512]{2,1,0:T(8,128)(2,1)} %param.31), channel_id=1, source_target_pairs={{8,0},{12,4},{16,8},{20,12},{24,16},{28,20},{9,1},{13,5},{17,9},{2... | collective-permute-start | bytes 98312 | tf_op jit(solution)/shard_map/ppermute | solution.py:28
  12.9 55.5 %collective-permute-start.4 = (bf16[2,32,512]{2,1,0:T(8,128)(2,1)}, bf16[2,32,512]{2,1,0:T(8,128)(2,1)}, u32[]{:S(2)}, u32[]{:S(2)}) collective-permute-start(bf16[2,32,512]{2,1,0:T(8,128)(2,1)} %param.30), channel_id=1, source_target_pairs={{0,4},{4,8},{8,12},{12,16},{16,20},{20,24},{24,28},{1,5},{5,9},{9,... | collective-permute-start | bytes 196616 | tf_op jit(solution)/shard_map/ppermute | solution.py:17
  23.1 21.9 %copy-start.10 = (pred[4,128]{1,0:T(4,128)(4,1)}, pred[4,128]{1,0:T(4,128)(4,1)S(1)}, u32[]{:S(2)}) copy-start(pred[4,128]{1,0:T(4,128)(4,1)S(1)} %iota_compare_fusion.8) | copy-start | bytes 1540
  23.8 21.9 %copy-start.11 = (pred[2,128]{1,0:T(4,128)(4,1)}, pred[2,128]{1,0:T(4,128)(4,1)S(1)}, u32[]{:S(2)}) copy-start(pred[2,128]{1,0:T(4,128)(4,1)S(1)} %iota_compare_fusion.10) | copy-start | bytes 772
  23.8 8.3 %copy-start.4 = (bf16[4,128,512]{2,1,0:T(8,128)(2,1)S(1)}, bf16[4,128,512]{2,1,0:T(8,128)(2,1)}, u32[]{:S(2)}) copy-start(bf16[4,128,512]{2,1,0:T(8,128)(2,1)} %param.25) | copy-start | bytes 1572868
  29.4 25.5 %copy-start.12 = (pred[2,12]{1,0:T(4,128)(4,1)}, pred[2,12]{1,0:T(4,128)(4,1)S(1)}, u32[]{:S(2)}) copy-start(pred[2,12]{1,0:T(4,128)(4,1)S(1)} %broadcast_compare_fusion.3) | copy-start | bytes 76
  32.2 60.3 %copy-start.1 = (bf16[4,32,512]{2,1,0:T(8,128)(2,1)}, bf16[4,32,512]{2,1,0:T(8,128)(2,1)S(1)}, u32[]{:S(2)}) copy-start(bf16[4,32,512]{2,1,0:T(8,128)(2,1)S(1)} %convolution_convert_fusion) | copy-start | bytes 393220
  32.2 25.1 %copy-start.2 = (bf16[2,512,512]{2,1,0:T(8,128)(2,1)S(1)}, bf16[2,512,512]{2,1,0:T(8,128)(2,1)}, u32[]{:S(2)}) copy-start(bf16[2,512,512]{2,1,0:T(8,128)(2,1)} %param.23) | copy-start | bytes 3145732
  32.5 41.4 %collective-permute-start.5 = (bf16[2,32,512]{2,1,0:T(8,128)(2,1)}, bf16[2,32,512]{2,1,0:T(8,128)(2,1)}, u32[]{:S(2)}, u32[]{:S(2)}) collective-permute-start(bf16[2,32,512]{2,1,0:T(8,128)(2,1)} %param.30), channel_id=1, source_target_pairs={{4,0},{8,4},{12,8},{16,12},{20,16},{24,20},{28,24},{5,1},{9,5},{13... | collective-permute-start | bytes 196616 | tf_op jit(solution)/shard_map/ppermute | solution.py:20
  34.5 19.4 %collective-permute-start.1 = (f32[4,32,128]{2,1,0:T(8,128)S(1)}, f32[4,32,128]{2,1,0:T(8,128)}, u32[]{:S(2)}, u32[]{:S(2)}) collective-permute-start(f32[4,32,128]{2,1,0:T(8,128)S(1)} %convolution_select_fusion), channel_id=1, source_target_pairs={{4,0},{8,4},{12,8},{16,12},{20,16},{24,20},{28,24},{5,1},{9,5},{13... | collective-permute-start | bytes 196616 | tf_op jit(solution)/shard_map/ppermute | solution.py:20
  37.0 17.0 %collective-permute-start = (f32[4,32,128]{2,1,0:T(8,128)S(1)}, f32[4,32,128]{2,1,0:T(8,128)}, u32[]{:S(2)}, u32[]{:S(2)}) collective-permute-start(f32[4,32,128]{2,1,0:T(8,128)S(1)} %convolution_select_fusion), channel_id=1, source_target_pairs={{0,4},{4,8},{8,12},{12,16},{16,20},{20,24},{24,28},{1,5},{5,9},{9,... | collective-permute-start | bytes 196616 | tf_op jit(solution)/shard_map/ppermute | solution.py:17
  43.4 47.2 %collective-permute-start.12 = (bf16[4,32,512]{2,1,0:T(8,128)(2,1)S(1)}, bf16[4,32,512]{2,1,0:T(8,128)(2,1)}, u32[]{:S(2)}, u32[]{:S(2)}) collective-permute-start(bf16[4,32,512]{2,1,0:T(8,128)(2,1)S(1)} %convolution_convert_fusion), channel_id=1, source_target_pairs={{0,3},{1,0},{2,1},{3,2},{4,7},{5,4},{6,5},{7,6},{8,11},{9,8},{10,9... | collective-permute-start | bytes 393224 | tf_op jit(solution)/shard_map/ppermute | solution.py:172
  45.0 0.7 copy-start.6
  46.5 7.1 %all-to-all-start.1 = ((bf16[4,2,1024]{2,1,0:T(2,128)(2,1)}), bf16[4,2,1024]{2,1,0:T(2,128)(2,1)S(1)}, u32[]{:S(2)}, u32[]{:S(2)}) async-start(bf16[4,2,1024]{2,1,0:T(2,128)(2,1)} %reshape.647), calls=%async_computation.1 | async-start | bytes 32768 | tf_op jit(solution)/shard_map/all_to_all | solution.py:181
  53.9 31.1 %collective-permute-start.10 = (bf16[4,32,512]{2,1,0:T(8,128)(2,1)S(1)}, bf16[4,32,512]{2,1,0:T(8,128)(2,1)}, u32[]{:S(2)}, u32[]{:S(2)}) collective-permute-start(bf16[4,32,512]{2,1,0:T(8,128)(2,1)S(1)} %convolution_convert_fusion), channel_id=1, source_target_pairs={{0,1},{1,2},{2,3},{3,0},{4,5},{5,6},{6,7},{7,4},{8,9},{9,10},{10,1... | collective-permute-start | bytes 393224 | tf_op jit(solution)/shard_map/ppermute | solution.py:170
  58.6 28.1 %copy-start.3 = (bf16[2,32,512]{2,1,0:T(8,128)(2,1)}, bf16[2,32,512]{2,1,0:T(8,128)(2,1)S(1)}, u32[]{:S(2)}) copy-start(bf16[2,32,512]{2,1,0:T(8,128)(2,1)S(1)} %convolution_convert_fusion.1) | copy-start | bytes 196612
  58.6 17.3 %copy-start.7 = (f32[32,128,4]{1,2,0:T(4,128)S(1)}, f32[32,128,4]{1,2,0:T(4,128)}, u32[]{:S(2)}) copy-start(f32[32,128,4]{1,2,0:T(4,128)} %convolution_bitcast_fusion.2) | copy-start | bytes 196612
  61.1 26.6 %copy-start.5 = (bf16[1,512,512]{2,1,0:T(8,128)(2,1)S(1)}, bf16[1,512,512]{2,1,0:T(8,128)(2,1)}, u32[]{:S(2)}) copy-start(bf16[1,512,512]{2,1,0:T(8,128)(2,1)} %param.24) | copy-start | bytes 1572868
  61.1 24.0 %collective-permute-start.3 = (f32[2,32,640]{2,0,1:T(2,128)}, f32[2,32,640]{2,0,1:T(2,128)}, u32[]{:S(2)}, u32[]{:S(2)}) collective-permute-start(f32[2,32,640]{2,0,1:T(2,128)} %constant_dynamic-update-slice_fusion), channel_id=1, source_target_pairs={{4,0},{8,4},{12,8},{16,12},{20,16},{24,20},{28,24},{5,1},{9,5},{13... | collective-permute-start | bytes 491528 | tf_op jit(solution)/shard_map/ppermute | solution.py:20
  68.4 16.6 %collective-permute-start.2 = (f32[2,32,640]{2,0,1:T(2,128)}, f32[2,32,640]{2,0,1:T(2,128)}, u32[]{:S(2)}, u32[]{:S(2)}) collective-permute-start(f32[2,32,640]{2,0,1:T(2,128)} %constant_dynamic-update-slice_fusion), channel_id=1, source_target_pairs={{0,4},{4,8},{8,12},{12,16},{16,20},{20,24},{24,28},{1,5},{5,9},{9,... | collective-permute-start | bytes 491528 | tf_op jit(solution)/shard_map/ppermute | solution.py:17
  74.9 11.8 %copy-start.13 = (pred[6]{0:T(512)(128)(4,1)S(1)}, pred[6]{0:T(512)(128)(4,1)}, u32[]{:S(2)}) copy-start(pred[6]{0:T(512)(128)(4,1)} %select_compare_fusion) | copy-start | bytes 22
  74.9 11.8 %copy-start.14 = (s32[6]{0:T(128)S(1)}, s32[6]{0:T(128)}, u32[]{:S(2)}) copy-start(s32[6]{0:T(128)} %broadcast_select_fusion.1) | copy-start | bytes 76
  74.9 12.8 %copy-start.8 = (bf16[1,32,512]{2,1,0:T(8,128)(2,1)S(1)}, bf16[1,32,512]{2,1,0:T(8,128)(2,1)}, u32[]{:S(2)}) copy-start(bf16[1,32,512]{2,1,0:T(8,128)(2,1)} %param.29) | copy-start | bytes 98308
  77.4 7.2 %all-to-all-start = ((bf16[4,2,2048]{2,1,0:T(2,128)(2,1)}), bf16[4,2,2048]{2,1,0:T(2,128)(2,1)S(1)}, u32[]{:S(2)}, u32[]{:S(2)}) async-start(bf16[4,2,2048]{2,1,0:T(2,128)(2,1)} %reshape.645), calls=%async_computation | async-start | bytes 65536 | tf_op jit(solution)/shard_map/all_to_all | solution.py:178
  85.0 4.7 %collective-permute-start.11 = (bf16[4,32,512]{2,1,0:T(8,128)(2,1)}, bf16[4,32,512]{2,1,0:T(8,128)(2,1)S(1)}, u32[]{:S(2)}, u32[]{:S(2)}) collective-permute-start(bf16[4,32,512]{2,1,0:T(8,128)(2,1)} %collective-permute-done.10), channel_id=1, source_target_pairs={{0,1},{1,2},{2,3},{3,0},{4,5},{5,6},{6,7},{7,4},{8,9},{9,10},{10,1... | collective-permute-start | bytes 393224 | tf_op jit(solution)/shard_map/ppermute | solution.py:170
